TPU v7x, 256 devices: a whole 4x4x8 slice. The times are simulated.
256 devices in a mesh: rows: 8 (over y, z_hi), cols: 32 (over x, z_lo, core).
Axes of the slice: x: 4, y: 4, z: 8 (z_hi: 2, z_lo: 4; z = z_hi * 4 + z_lo), core: 2. Of those that a mesh axis runs over, the one named last changes fastest.
Arguments:
- covariance: float32 [8192, 8192], P('rows', 'cols'), may hold values from -6 to 6
- zonal: float32 [64, 128, 128], P('rows'), may hold values from -0.5 to 0.5
- stencil: float32 [64, 3, 128], P('rows'), may hold values from -0.5 to 1.1, as said below
Outputs:
- lagged: float32 [8192, 8192], P('rows', 'cols')
Inputs may be any that keep to these rules, and one draw needn't show every extreme that they name: `stencil`: component 0 lies in 0.7 to 1.1, components 1 and 2 in -0.5 to 0.5.
All inputs are finite; a program needn't handle non-finite values.
Results may differ from a plain program's by a relative error of at most 0.0003.
Values sent between devices are 32-bit elements; how exact they have to be, the bound alone decides.
A program may use at most 64 MiB of HBM per device.

v0:
```python
import jax
import jax.numpy as jnp
from jax import lax
from jax.sharding import PartitionSpec as P

STEPS = 3
LAGS = 3


def from_root(value, axis, root):
    mine = lax.axis_index(axis) == root
    return lax.psum(jnp.where(mine, value, jnp.zeros_like(value)), axis)


def with_halo(block, sides, width):
    for axis, dim in sides:
        count = lax.axis_size(axis)
        forward = [(i, i + 1) for i in range(count - 1)]
        backward = [(target, source) for source, target in forward]
        low = lax.ppermute(
            lax.slice_in_dim(block, block.shape[dim] - width, None, axis=dim), axis, forward
        )
        high = lax.ppermute(lax.slice_in_dim(block, 0, width, axis=dim), axis, backward)
        block = jnp.concatenate([low, block, high], axis=dim)
    return block


def rows_local(extended, operator):
    latitudes = operator.shape[0]
    longitudes = operator.shape[2]
    zonal_mats = operator[:, :longitudes]
    weights = operator[:, longitudes:]
    blocks = extended.reshape(latitudes + 2, longitudes, extended.shape[1])
    mixed = (
        weights[:, 0, :, None] * blocks[1:-1]
        + weights[:, 1, :, None] * blocks[2:]
        + weights[:, 2, :, None] * blocks[:-2]
    )
    turned = jnp.einsum("lij,ljc->lic", zonal_mats, mixed, precision=lax.Precision.HIGHEST)
    return turned.reshape(latitudes * longitudes, extended.shape[1])


def cols_local(extended, operator):
    latitudes = operator.shape[0]
    longitudes = operator.shape[2]
    zonal_mats = operator[:, :longitudes]
    weights = operator[:, longitudes:]
    blocks = extended.reshape(extended.shape[0], latitudes + 2, longitudes)
    mixed = (
        weights[None, :, 0, :] * blocks[:, 1:-1]
        + weights[None, :, 1, :] * blocks[:, 2:]
        + weights[None, :, 2, :] * blocks[:, :-2]
    )
    turned = jnp.einsum("rlj,lij->rli", mixed, zonal_mats, precision=lax.Precision.HIGHEST)
    return turned.reshape(extended.shape[0], latitudes * longitudes)


def on_device(covariance, zonal, stencil):
    longitudes = zonal.shape[1]
    lat_rows = zonal.shape[0]
    row_count = lax.axis_size("rows")
    col_count = lax.axis_size("cols")
    ratio = col_count // row_count
    lat_cols = lat_rows // ratio
    operator = jnp.concatenate([zonal, stencil], axis=1)
    col_index = lax.axis_index("cols")
    owner = from_root(operator, "rows", col_index // ratio)
    col_operator = lax.dynamic_slice_in_dim(owner, col_index % ratio * lat_cols, lat_cols, 0)

    def left_phase(matrix, count):
        for inner in range(count):
            extended = with_halo(matrix, (("rows", 0),), longitudes)
            matrix = rows_local(extended, operator)
        return matrix

    current = left_phase(covariance, STEPS)
    for repeat in range(STEPS):
        right_extended = with_halo(current, (("cols", 1),), longitudes)
        current = cols_local(right_extended, col_operator)
    tile_cols = current.shape[1]
    piece = tile_cols // row_count
    moved = lax.all_to_all(
        lax.all_to_all(current, "rows", split_axis=1, concat_axis=0, tiled=True),
        "cols",
        split_axis=0,
        concat_axis=1,
        tiled=True,
    )
    turned = moved.T.reshape(col_count, piece, tile_cols)
    settled = lax.all_to_all(turned, "rows", split_axis=0, concat_axis=1, tiled=True)
    current = settled.reshape(ratio * row_count * piece, tile_cols)
    current = left_phase(current, LAGS)
    return current


def solution(mesh):
    placed = (P("rows", "cols"), P("rows", None, None), P("rows", None, None))
    return jax.shard_map(
        on_device, mesh=mesh, in_specs=placed, out_specs=P("rows", "cols"), check_vma=False
    )
```

profile of v0, /device:TPU:8, one launch (start us, length us, event | category | flops | bytes accessed | tf_op | source)
XLA Modules:
  0.0 384.9 jit_solution(16931720801505099183)
XLA Ops:
  7.6 9.0 %collective-permute-start = (f32[128,256]{1,0:T(8,128)S(1)}, f32[128,256]{1,0:T(8,128)S(1)}, u32[]{:S(2)}, u32[]{:S(2)}) collective-permute-start(f32[128,256]{1,0:T(8,128)S(1)} %get-tuple-element.33), channel_id=1, source_target_pairs={{32,0},{64,32},{96,64},{128,96},{160,128},{192,160},{224,192},{33,... | collective-permute-start | bytes 393224 | tf_op jit(solution)/shard_map/ppermute | solution.py:23
  19.4 2.7 collective-permute-done
  22.1 8.2 %collective-permute-done.1 = f32[128,256]{1,0:T(8,128)S(1)} collective-permute-done((f32[128,256]{1,0:T(8,128)S(1)}, f32[128,256]{1,0:T(8,128)S(1)}, u32[]{:S(2)}, u32[]{:S(2)}) %collective-permute-start.1) | collective-permute-done | bytes 131104 | tf_op jit(solution)/shard_map/ppermute | solution.py:20
  35.4 7.8 %collective-permute-start.3 = (f32[128,256]{1,0:T(8,128)S(1)}, f32[128,256]{1,0:T(8,128)S(1)}, u32[]{:S(2)}, u32[]{:S(2)}) collective-permute-start(f32[128,256]{1,0:T(8,128)S(1)} %get-tuple-element.30), channel_id=1, source_target_pairs={{0,32},{32,64},{64,96},{96,128},{128,160},{160,192},{192,224},{1,3... | collective-permute-start | bytes 393224 | tf_op jit(solution)/shard_map/ppermute | solution.py:20
  44.9 4.0 %collective-permute-done.3 = f32[128,256]{1,0:T(8,128)S(1)} collective-permute-done((f32[128,256]{1,0:T(8,128)S(1)}, f32[128,256]{1,0:T(8,128)S(1)}, u32[]{:S(2)}, u32[]{:S(2)}) %collective-permute-start.3) | collective-permute-done | bytes 131104 | tf_op jit(solution)/shard_map/ppermute | solution.py:20
  52.7 8.0 %collective-permute-start.5 = (f32[128,256]{1,0:T(8,128)S(1)}, f32[128,256]{1,0:T(8,128)S(1)}, u32[]{:S(2)}, u32[]{:S(2)}) collective-permute-start(f32[128,256]{1,0:T(8,128)S(1)} %get-tuple-element.26), channel_id=1, source_target_pairs={{0,32},{32,64},{64,96},{96,128},{128,160},{160,192},{192,224},{1,3... | collective-permute-start | bytes 393224 | tf_op jit(solution)/shard_map/ppermute | solution.py:20
  62.0 4.9 %collective-permute-done.5 = f32[128,256]{1,0:T(8,128)S(1)} collective-permute-done((f32[128,256]{1,0:T(8,128)S(1)}, f32[128,256]{1,0:T(8,128)S(1)}, u32[]{:S(2)}, u32[]{:S(2)}) %collective-permute-start.5) | collective-permute-done | bytes 131104 | tf_op jit(solution)/shard_map/ppermute | solution.py:20
  71.8 109.5 %all-reduce.2.cloned.1.call-done = f32[8,131,128]{2,1,0:T(8,128)} async-done(((f32[8,131,128]{2,1,0:T(8,128)}), f32[8,131,128]{2,1,0:T(8,128)}) %all-reduce.2.cloned.1.call-update) | async-done | bytes 536592 | tf_op jit(solution)/shard_map/psum | solution.py:12
  187.5 3.7 collective-permute-done.9
  192.7 14.5 %collective-permute-start.10 = (f32[1024,128]{0,1:T(8,128)S(1)}, f32[1024,128]{0,1:T(8,128)S(1)}, u32[]{:S(2)}, u32[]{:S(2)}) collective-permute-start(f32[1024,128]{0,1:T(8,128)S(1)} %get-tuple-element.17), channel_id=1, source_target_pairs={{0,1},{1,2},{2,3},{3,4},{4,5},{5,6},{6,7},{7,8},{8,9},{9,10},{10,1... | collective-permute-start | bytes 1572872 | tf_op jit(solution)/shard_map/ppermute | solution.py:20
  212.6 18.0 %all_to_all.50 = f32[1024,8,32]{0,2,1:T(8,128)S(1)} all-to-all(f32[1024,8,32]{0,2,1:T(8,128)S(1)} %bitcast.127), channel_id=1, replica_groups=mesh['rows'=8,'cols'=32] {'rows'}, dimensions={1} | all-to-all | bytes 2097152 | tf_op jit(solution)/shard_map/all_to_all | solution.py:83
  232.1 58.2 %all_to_all.51 = f32[32,256,32]{1,2,0:T(8,128)S(1)} all-to-all(f32[32,256,32]{1,2,0:T(8,128)S(1)} %copy.34), channel_id=1, replica_groups=mesh['rows'=8,'cols'=32] {'cols'}, dimensions={0} | all-to-all | bytes 2097152 | tf_op jit(solution)/shard_map/all_to_all | solution.py:82
  290.3 32.6 %all_to_all.52 = f32[32,32,256]{2,1,0:T(8,128)S(1)} all-to-all(f32[32,32,256]{2,1,0:T(8,128)S(1)} %bitcast.125), channel_id=1, replica_groups=mesh['rows'=8,'cols'=32] {'rows'}, dimensions={0} | all-to-all | bytes 2097152 | tf_op jit(solution)/shard_map/all_to_all | solution.py:90
  323.1 6.5 %collective-permute-start.12 = (f32[128,256]{1,0:T(8,128)S(1)}, f32[128,256]{1,0:T(8,128)S(1)}, u32[]{:S(2)}, u32[]{:S(2)}) collective-permute-start(f32[128,256]{1,0:T(8,128)S(1)} %get-tuple-element.15), channel_id=1, source_target_pairs={{32,0},{64,32},{96,64},{128,96},{160,128},{192,160},{224,192},{33,... | collective-permute-start | bytes 393224 | tf_op jit(solution)/shard_map/ppermute | solution.py:23
  329.6 3.5 collective-permute-start.13
  333.1 2.8 collective-permute-done.12
  335.9 5.4 %collective-permute-done.13 = f32[128,256]{1,0:T(8,128)S(1)} collective-permute-done((f32[128,256]{1,0:T(8,128)S(1)}, f32[128,256]{1,0:T(8,128)S(1)}, u32[]{:S(2)}, u32[]{:S(2)}) %collective-permute-start.13) | collective-permute-done | bytes 131104 | tf_op jit(solution)/shard_map/ppermute | solution.py:20
  343.1 3.8 collective-permute-start.14
  346.9 6.0 %collective-permute-start.15 = (f32[128,256]{1,0:T(8,128)S(1)}, f32[128,256]{1,0:T(8,128)S(1)}, u32[]{:S(2)}, u32[]{:S(2)}) collective-permute-start(f32[128,256]{1,0:T(8,128)S(1)} %get-tuple-element.12), channel_id=1, source_target_pairs={{0,32},{32,64},{64,96},{96,128},{128,160},{160,192},{192,224},{1,3... | collective-permute-start | bytes 393224 | tf_op jit(solution)/shard_map/ppermute | solution.py:20
  355.0 3.6 collective-permute-done.15
  360.4 3.4 collective-permute-start.16
  363.8 6.4 %collective-permute-start.17 = (f32[128,256]{1,0:T(8,128)S(1)}, f32[128,256]{1,0:T(8,128)S(1)}, u32[]{:S(2)}, u32[]{:S(2)}) collective-permute-start(f32[128,256]{1,0:T(8,128)S(1)} %get-tuple-element.8), channel_id=1, source_target_pairs={{0,32},{32,64},{64,96},{96,128},{128,160},{160,192},{192,224},{1,3... | collective-permute-start | bytes 393224 | tf_op jit(solution)/shard_map/ppermute | solution.py:20
  370.2 3.8 %collective-permute-done.16 = f32[128,256]{1,0:T(8,128)S(1)} collective-permute-done((f32[128,256]{1,0:T(8,128)S(1)}, f32[128,256]{1,0:T(8,128)S(1)}, u32[]{:S(2)}, u32[]{:S(2)}) %collective-permute-start.16) | collective-permute-done | bytes 131104 | tf_op jit(solution)/shard_map/ppermute | solution.py:23
  375.7 2.4 fusion.15
  (62 shorter events, 42.4 us)
Async XLA Ops:
  6.5 25.3 %copy-start.1 = (f32[1024,256]{1,0:T(8,128)S(1)}, f32[1024,256]{1,0:T(8,128)}, u32[]{:S(2)}) copy-start(f32[1024,256]{1,0:T(8,128)} %param.3) | copy-start | bytes 3145732
  6.5 25.3 %copy-start = (f32[8,128,128]{2,1,0:T(8,128)S(1)}, f32[8,128,128]{2,1,0:T(8,128)}, u32[]{:S(2)}) copy-start(f32[8,128,128]{2,1,0:T(8,128)} %param.4) | copy-start | bytes 1572868
  6.5 174.7 %all-reduce.2.cloned.1.call-start = ((), (), s32[]{:S(2)}) async-start(), calls=%async_computation.3 | async-start | bytes 1114112 | tf_op jit(solution)/shard_map/psum | solution.py:12
  7.6 14.4 %collective-permute-start = (f32[128,256]{1,0:T(8,128)S(1)}, f32[128,256]{1,0:T(8,128)S(1)}, u32[]{:S(2)}, u32[]{:S(2)}) collective-permute-start(f32[128,256]{1,0:T(8,128)S(1)} %get-tuple-element.33), channel_id=1, source_target_pairs={{32,0},{64,32},{96,64},{128,96},{160,128},{192,160},{224,192},{33,... | collective-permute-start | bytes 393224 | tf_op jit(solution)/shard_map/ppermute | solution.py:23
  16.6 13.6 %collective-permute-start.1 = (f32[128,256]{1,0:T(8,128)S(1)}, f32[128,256]{1,0:T(8,128)S(1)}, u32[]{:S(2)}, u32[]{:S(2)}) collective-permute-start(f32[128,256]{1,0:T(8,128)S(1)} %get-tuple-element.34), channel_id=1, source_target_pairs={{0,32},{32,64},{64,96},{96,128},{128,160},{160,192},{192,224},{1,3... | collective-permute-start | bytes 393224 | tf_op jit(solution)/shard_map/ppermute | solution.py:20
  33.5 11.4 %collective-permute-start.2 = (f32[128,256]{1,0:T(8,128)S(1)}, f32[128,256]{1,0:T(8,128)S(1)}, u32[]{:S(2)}, u32[]{:S(2)}) collective-permute-start(f32[128,256]{1,0:T(8,128)S(1)} %get-tuple-element.29), channel_id=1, source_target_pairs={{32,0},{64,32},{96,64},{128,96},{160,128},{192,160},{224,192},{33,... | collective-permute-start | bytes 393224 | tf_op jit(solution)/shard_map/ppermute | solution.py:23
  35.4 13.5 %collective-permute-start.3 = (f32[128,256]{1,0:T(8,128)S(1)}, f32[128,256]{1,0:T(8,128)S(1)}, u32[]{:S(2)}, u32[]{:S(2)}) collective-permute-start(f32[128,256]{1,0:T(8,128)S(1)} %get-tuple-element.30), channel_id=1, source_target_pairs={{0,32},{32,64},{64,96},{96,128},{128,160},{160,192},{192,224},{1,3... | collective-permute-start | bytes 393224 | tf_op jit(solution)/shard_map/ppermute | solution.py:20
  49.1 11.6 %copy-start.3 = (f32[8,3,128]{2,0,1:T(8,128)S(1)}, f32[8,3,128]{2,0,1:T(8,128)}, u32[]{:S(2)}) copy-start(f32[8,3,128]{2,0,1:T(8,128)} %param.5) | copy-start | bytes 36868
  50.8 11.2 %collective-permute-start.4 = (f32[128,256]{1,0:T(8,128)S(1)}, f32[128,256]{1,0:T(8,128)S(1)}, u32[]{:S(2)}, u32[]{:S(2)}) collective-permute-start(f32[128,256]{1,0:T(8,128)S(1)} %get-tuple-element.25), channel_id=1, source_target_pairs={{32,0},{64,32},{96,64},{128,96},{160,128},{192,160},{224,192},{33,... | collective-permute-start | bytes 393224 | tf_op jit(solution)/shard_map/ppermute | solution.py:23
  52.7 14.2 %collective-permute-start.5 = (f32[128,256]{1,0:T(8,128)S(1)}, f32[128,256]{1,0:T(8,128)S(1)}, u32[]{:S(2)}, u32[]{:S(2)}) collective-permute-start(f32[128,256]{1,0:T(8,128)S(1)} %get-tuple-element.26), channel_id=1, source_target_pairs={{0,32},{32,64},{64,96},{96,128},{128,160},{160,192},{192,224},{1,3... | collective-permute-start | bytes 393224 | tf_op jit(solution)/shard_map/ppermute | solution.py:20
  69.1 112.9 %collective-permute-start.6 = (f32[1024,128]{0,1:T(8,128)S(1)}, f32[1024,128]{0,1:T(8,128)S(1)}, u32[]{:S(2)}, u32[]{:S(2)}) collective-permute-start(f32[1024,128]{0,1:T(8,128)S(1)} %get-tuple-element.21), channel_id=1, source_target_pairs={{0,1},{1,2},{2,3},{3,4},{4,5},{5,6},{6,7},{7,8},{8,9},{9,10},{10,1... | collective-permute-start | bytes 1572872 | tf_op jit(solution)/shard_map/ppermute | solution.py:20
  70.5 111.6 %collective-permute-start.7 = (f32[1024,128]{0,1:T(8,128)S(1)}, f32[1024,128]{0,1:T(8,128)}, u32[]{:S(2)}, u32[]{:S(2)}) collective-permute-start(f32[1024,128]{0,1:T(8,128)S(1)} %get-tuple-element.22), channel_id=1, source_target_pairs={{1,0},{2,1},{3,2},{4,3},{5,4},{6,5},{7,6},{8,7},{9,8},{10,9},{11,1... | collective-permute-start | bytes 1572872 | tf_op jit(solution)/shard_map/ppermute | solution.py:23
  182.0 1.3 copy-start.2
  184.6 2.8 collective-permute-start.8
  186.0 5.2 %collective-permute-start.9 = (f32[1024,128]{0,1:T(8,128)S(1)}, f32[1024,128]{0,1:T(8,128)S(1)}, u32[]{:S(2)}, u32[]{:S(2)}) collective-permute-start(f32[1024,128]{0,1:T(8,128)S(1)} %get-tuple-element.20), channel_id=1, source_target_pairs={{1,0},{2,1},{3,2},{4,3},{5,4},{6,5},{7,6},{8,7},{9,8},{10,9},{11,1... | collective-permute-start | bytes 1572872 | tf_op jit(solution)/shard_map/ppermute | solution.py:23
  192.7 16.0 %collective-permute-start.10 = (f32[1024,128]{0,1:T(8,128)S(1)}, f32[1024,128]{0,1:T(8,128)S(1)}, u32[]{:S(2)}, u32[]{:S(2)}) collective-permute-start(f32[1024,128]{0,1:T(8,128)S(1)} %get-tuple-element.17), channel_id=1, source_target_pairs={{0,1},{1,2},{2,3},{3,4},{4,5},{5,6},{6,7},{7,8},{8,9},{9,10},{10,1... | collective-permute-start | bytes 1572872 | tf_op jit(solution)/shard_map/ppermute | solution.py:20
  207.3 3.8 collective-permute-start.11
  323.1 12.8 %collective-permute-start.12 = (f32[128,256]{1,0:T(8,128)S(1)}, f32[128,256]{1,0:T(8,128)S(1)}, u32[]{:S(2)}, u32[]{:S(2)}) collective-permute-start(f32[128,256]{1,0:T(8,128)S(1)} %get-tuple-element.15), channel_id=1, source_target_pairs={{32,0},{64,32},{96,64},{128,96},{160,128},{192,160},{224,192},{33,... | collective-permute-start | bytes 393224 | tf_op jit(solution)/shard_map/ppermute | solution.py:23
  329.6 11.7 %collective-permute-start.13 = (f32[128,256]{1,0:T(8,128)S(1)}, f32[128,256]{1,0:T(8,128)S(1)}, u32[]{:S(2)}, u32[]{:S(2)}) collective-permute-start(f32[128,256]{1,0:T(8,128)S(1)} %get-tuple-element.16), channel_id=1, source_target_pairs={{0,32},{32,64},{64,96},{96,128},{128,160},{160,192},{192,224},{1,3... | collective-permute-start | bytes 393224 | tf_op jit(solution)/shard_map/ppermute | solution.py:20
  343.1 11.9 %collective-permute-start.14 = (f32[128,256]{1,0:T(8,128)S(1)}, f32[128,256]{1,0:T(8,128)S(1)}, u32[]{:S(2)}, u32[]{:S(2)}) collective-permute-start(f32[128,256]{1,0:T(8,128)S(1)} %get-tuple-element.11), channel_id=1, source_target_pairs={{32,0},{64,32},{96,64},{128,96},{160,128},{192,160},{224,192},{33,... | collective-permute-start | bytes 393224 | tf_op jit(solution)/shard_map/ppermute | solution.py:23
  346.9 11.8 %collective-permute-start.15 = (f32[128,256]{1,0:T(8,128)S(1)}, f32[128,256]{1,0:T(8,128)S(1)}, u32[]{:S(2)}, u32[]{:S(2)}) collective-permute-start(f32[128,256]{1,0:T(8,128)S(1)} %get-tuple-element.12), channel_id=1, source_target_pairs={{0,32},{32,64},{64,96},{96,128},{128,160},{160,192},{192,224},{1,3... | collective-permute-start | bytes 393224 | tf_op jit(solution)/shard_map/ppermute | solution.py:20
  360.4 13.6 %collective-permute-start.16 = (f32[128,256]{1,0:T(8,128)S(1)}, f32[128,256]{1,0:T(8,128)S(1)}, u32[]{:S(2)}, u32[]{:S(2)}) collective-permute-start(f32[128,256]{1,0:T(8,128)S(1)} %get-tuple-element.7), channel_id=1, source_target_pairs={{32,0},{64,32},{96,64},{128,96},{160,128},{192,160},{224,192},{33,... | collective-permute-start | bytes 393224 | tf_op jit(solution)/shard_map/ppermute | solution.py:23
  363.8 11.7 %collective-permute-start.17 = (f32[128,256]{1,0:T(8,128)S(1)}, f32[128,256]{1,0:T(8,128)S(1)}, u32[]{:S(2)}, u32[]{:S(2)}) collective-permute-start(f32[128,256]{1,0:T(8,128)S(1)} %get-tuple-element.8), channel_id=1, source_target_pairs={{0,32},{32,64},{64,96},{96,128},{128,160},{160,192},{192,224},{1,3... | collective-permute-start | bytes 393224 | tf_op jit(solution)/shard_map/ppermute | solution.py:20
Sparse Core Ops, SparseCore 0:
  61.8 119.4 all-reduce.1
where the time goes:
time: 392 us; the launch traced here: 385 us
  waiting for transfers between devices  157 us (40%)
  blocking collectives  109 us (28%)
  starting transfers between devices  81.2 us (21%)
  matrix products  14.2 us (4%)
  between operations  13.9 us (4%)
  other arithmetic  4.99 us (1%)
  local copies, waits for them, and re-layouts  4.95 us (1%)
    psum x1, waiting for transfers between devices, from_root(): return lax.psum(jnp.where(mine, value, jnp.zeros_like(value)), axis)  109 us
    all_to_all x1, blocking collectives, on_device(): lax.all_to_all(lax.all_to_all(current, 'rows', split_axis=1, concat_axis=...  58.2 us
    ppermute x9, starting transfers between devices, with_halo(): lax.ppermute(lax.slice_in_dim(block, block.shape[dim] - width, None, axis...  50.9 us
    all_to_all x1, blocking collectives, on_device(): lax.all_to_all(turned, 'rows', split_axis=0, concat_axis=1, tiled=True)  32.6 us
    ppermute x9, starting transfers between devices, with_halo(): lax.ppermute(lax.slice_in_dim(block, 0, width, axis=dim), axis, backward)  30.3 us
    ppermute x9, waiting for transfers between devices, with_halo(): lax.ppermute(lax.slice_in_dim(block, block.shape[dim] - width, None, axis...  27.9 us
    ppermute x9, waiting for transfers between devices, with_halo(): lax.ppermute(lax.slice_in_dim(block, 0, width, axis=dim), axis, backward)  19.5 us
    all_to_all x1, blocking collectives, on_device(): lax.all_to_all(current, 'rows', split_axis=1, concat_axis=0, tiled=True)  18 us
  transfers between devices with their start and end apart: 19, of which 17 were waited for; matrix products, arithmetic and copies ran while one was open for 1% of the time, Pallas kernels for 0%

commit v1 on v0

v1 whole, which is shorter than its diff:
```python
import jax
import jax.numpy as jnp
from jax import lax
from jax.experimental import pallas as pl
from jax.experimental.pallas import tpu as pltpu
from jax.sharding import PartitionSpec as P

MESH = pl.DeviceIdType.MESH
N = 128
F32, BF16 = jnp.float32, jnp.bfloat16


def div(a, b):
    return lax.div(a, jnp.int32(b))


def rem(a, b):
    return lax.rem(a, jnp.int32(b))


def device(x, y, z, core):
    return (y * 2 + div(z, 4), x * 8 + rem(z, 4) * 2 + core)


def rows(first, count):
    return pl.ds(pl.multiple_of(first * N, N), count * N)


def kernel(cov, zonal, stencil, out, op, b_hi, b_lo, x1, x2, x3, ya, yb, ts, es,
           e_send, e_recv, o_send, o_recv, h_send, h_recv, t_send, t_recv, f_send, g_send, g_recv):
    row, col = lax.axis_index("rows"), lax.axis_index("cols")
    y, zh = div(row, 2), rem(row, 2)
    x, zl, core = div(col, 8), div(rem(col, 8), 2), rem(col, 2)
    z = zh * 4 + zl
    me16 = z * 2 + core
    partner = (row + 1 - 2 * zh, col)
    piece = x * 2 + core
    other = 1 - zh
    edge_chip = (zl == 0) | (zl == 3)
    diagonal = x == y
    clat = zl * 4 + core * 2 + zh

    def remote(src, dst, send, recv, dev):
        return pltpu.make_async_remote_copy(
            src_ref=src, dst_ref=dst, send_sem=send, recv_sem=recv, device_id=dev, device_id_type=MESH)

    for i in range(8):
        op[2 + 8 * zh + i, 0:N, :] = zonal[i]
        op[2 + 8 * zh + i, N:N + 3, :] = stencil[i]

    @pl.when(y == 0)
    def _():
        op[0:2] = jnp.zeros((2, N + 8, N), F32)
        for ref in (x1, x2, x3):
            ref[0:3 * N, :] = jnp.zeros((3 * N, N), F32)

    @pl.when(y == 3)
    def _():
        op[18:20] = jnp.zeros((2, N + 8, N), F32)
        for ref in (x1, x2, x3):
            ref[19 * N:22 * N, :] = jnp.zeros((3 * N, N), F32)

    barrier = pltpu.get_barrier_semaphore()

    def greet(dev):
        pl.semaphore_signal(barrier, inc=1, device_id=dev, device_id_type=MESH)

    greet(partner)
    near = jnp.where(zh == 0, jnp.where(zl < 2, 7, 4), jnp.where(zl < 2, 3, 0))
    greet(device(x, y, near, core))

    def greet_group(k, c):
        q = rem(piece + k, 8)
        greet(device(div(q, 2), y, z, rem(q, 2)))
        return c

    lax.fori_loop(1, 8, greet_group, 0)

    @pl.when(y > 0)
    def _():
        greet(device(x, y - 1, z, core))

    @pl.when(y < 3)
    def _():
        greet(device(x, y + 1, z, core))

    @pl.when(diagonal)
    def _():
        def same(k, c):
            d = rem(me16 + k, 16)
            greet(device(x, y, div(d, 2), rem(d, 2)))
            return c

        lax.fori_loop(1, 16, same, 0)

        def relayed(j, c):
            greet(device(x, rem(x + 1 + div(j, 8), 4), rem(j, 8), 1 - core))
            return c

        lax.fori_loop(0, 24, relayed, 0)

    @pl.when(jnp.logical_not(diagonal))
    def _():
        def direct(k, c):
            greet(device(y, x, k, core))
            return c

        lax.fori_loop(0, 8, direct, 0)
        greet(device(y, y, z, core))

    writes = (1 + 7 + jnp.where(edge_chip, 2, 0) + jnp.where(y > 0, 1, 0) + jnp.where(y < 3, 1, 0)
              + jnp.where(diagonal, 15 + 3, 16))
    pl.semaphore_wait(barrier, writes)

    theirs = pl.ds(pl.multiple_of(other * N, N), N)
    mine = pl.ds(pl.multiple_of(zh * N, N), N)
    swap_edge = remote(cov.at[rows(zh * 5, 3), theirs], x1.at[rows(3 + zh * 13, 3)],
                       e_send.at[0], e_recv.at[0], partner)
    swap_rest = remote(cov.at[rows(other * 3, 5), theirs], x1.at[rows(6 + zh * 5, 5)],
                       e_send.at[1], e_recv.at[1], partner)

    @pl.when(edge_chip)
    def _():
        for far in range(2):
            to = jnp.where(zl == 3, rem(z + 1 + far, 8), rem(z + 7 - far, 8))
            slot = 2 + 8 * zh + piece
            remote(op.at[slot], op.at[slot], o_send.at[far], o_recv.at[piece], device(x, y, to, core)).start()

    swap_edge.start()
    swap_rest.start()

    def border(stage, side, src, dst_first):
        dev = device(x, jnp.where(side == 0, y - 1, y + 1), z, core)
        return remote(src, dst_first, h_send.at[stage * 2 + side], h_recv.at[stage * 2 + side], dev)

    def has(side):
        return jnp.where(side == 0, y > 0, y < 3)

    @pl.when(has(zh))
    def _():
        border(0, zh, cov.at[rows(zh * 5, 3), mine], x1.at[rows(19 - 19 * zh, 3)]).start()

    x1[rows(3 + 8 * zh, 8), :] = cov[:, mine]

    slot = 2 + 8 * other + piece
    remote(op.at[slot], op.at[slot], o_send.at[0], o_recv.at[piece], partner).wait_recv()

    def share(k, c):
        q = rem(piece + k, 8)
        remote(op.at[slot], op.at[slot], o_send.at[1 + k], o_recv.at[piece], device(div(q, 2), y, z, rem(q, 2))).start()
        return c

    lax.fori_loop(1, 8, share, 0)

    def build(l, c):
        z_mat = op[l, 0:N, :]
        for part, comp in enumerate((2, 0, 1)):
            scaled = z_mat * op[l, N + comp:N + comp + 1, :]
            hi = scaled.astype(BF16)
            b_hi[l, :, part * N:(part + 1) * N] = hi
            b_lo[l, :, part * N:(part + 1) * N] = (scaled - hi.astype(F32)).astype(BF16)
        return c

    lax.fori_loop(2 + 8 * zh, 10 + 8 * zh, build, 0)

    swap_edge.wait_recv()

    @pl.when(has(other))
    def _():
        border(0, other, x1.at[rows(3 + 13 * other, 3)], x1.at[rows(19 - 19 * other, 3)]).start()

    def shared(k, c):
        q = rem(piece + k, 8)
        s = 2 + 8 * other + q
        remote(op.at[s], op.at[s], o_send.at[0], o_recv.at[q], partner).wait_recv()
        return c

    lax.fori_loop(1, 8, shared, 0)

    @pl.when(y > 0)
    def _():
        remote(op.at[pl.ds(2, 2)], op.at[pl.ds(18, 2)], o_send.at[9], o_recv.at[8],
               device(x, y - 1, z, core)).start()

    @pl.when(y < 3)
    def _():
        remote(op.at[pl.ds(16, 2)], op.at[pl.ds(0, 2)], o_send.at[10], o_recv.at[9],
               device(x, y + 1, z, core)).start()

    lax.fori_loop(2 + 8 * other, 10 + 8 * other, build, 0)

    @pl.when(y < 3)
    def _():
        remote(op.at[pl.ds(18, 2)], op.at[pl.ds(18, 2)], o_send.at[0], o_recv.at[8], partner).wait_recv()

    @pl.when(y > 0)
    def _():
        remote(op.at[pl.ds(0, 2)], op.at[pl.ds(0, 2)], o_send.at[0], o_recv.at[9], partner).wait_recv()

    lax.fori_loop(0, 2, build, 0)
    lax.fori_loop(18, 20, build, 0)

    def one(src, i):
        v = src[rows(i, 3), :]
        hi = v.astype(BF16)
        lo = (v - hi.astype(F32)).astype(BF16)
        bh = b_hi[i]
        acc = jnp.dot(bh, lo, preferred_element_type=F32)
        acc += jnp.dot(b_lo[i], hi, preferred_element_type=F32)
        return acc + jnp.dot(bh, hi, preferred_element_type=F32)

    def sweep(src, dst, first, last):
        def body(i, c):
            dst[rows(i + 1, 1), :] = one(src, i)
            return c

        lax.fori_loop(first + 2, last + 2, body, 0)

    def wait_borders(stage, ref):
        @pl.when(y < 3)
        def _():
            border(stage, 0, ref.at[rows(19, 3)], ref.at[rows(19, 3)]).wait_recv()

        @pl.when(y > 0)
        def _():
            border(stage, 1, ref.at[rows(0, 3)], ref.at[rows(0, 3)]).wait_recv()

    swap_rest.wait_recv()
    wait_borders(0, x1)
    sweep(x1, ya, -2, 18)
    sweep(ya, yb, -1, 17)

    def turn(lat, c):
        ts[lat] = one(yb, lat + 2).T
        return c

    lax.fori_loop(0, 16, turn, 0)

    def target(k):
        d = rem(me16 + k, 16)
        zt, ct = div(d, 2), rem(d, 2)
        lat = 8 * div(rem(zt, 4), 2) + 4 * rem(zt, 2) + 2 * ct + div(zt, 4)
        relay = jnp.logical_and(jnp.logical_not(diagonal), ct != core)
        dev = device(jnp.where(relay, x, y), x, zt, ct)
        slot = jnp.where(relay, 19 + rem(y + 3 - x, 4) * 8 + z, clat)
        return lat, slot, dev

    def send_block(k, c):
        lat, slot, dev = target(k)
        remote(ts.at[lat], x2.at[rows(slot + 3, 1)], t_send.at[k], t_recv.at[slot], dev).start()
        return c

    self_copy = pltpu.make_async_copy(
        ts.at[8 * div(zl, 2) + 4 * rem(zl, 2) + 2 * core + zh], x2.at[rows(clat + 3, 1)], t_recv.at[clat])

    @pl.when(diagonal)
    def _():
        self_copy.start()

    @pl.when(jnp.logical_not(diagonal))
    def _():
        send_block(0, 0)

    lax.fori_loop(1, 16, send_block, 0)

    def forward(j):
        zs = rem(j, 8)
        lat_from = rem(zs, 4) * 4 + (1 - core) * 2 + div(zs, 4)
        return remote(x2.at[rows(22 + j, 1)], x2.at[rows(lat_from + 3, 1)], f_send.at[j], t_recv.at[lat_from],
                      device(rem(x + 1 + div(j, 8), 4), x, z, core))

    def arrived(slot):
        remote(ts.at[0], x2.at[rows(slot + 3, 1)], t_send.at[0], t_recv.at[slot], partner).wait_recv()

    @pl.when(diagonal)
    def _():
        def pass_on(j, c):
            arrived(19 + j)
            forward(j).start()
            return c

        lax.fori_loop(0, 24, pass_on, 0)

    def arrive(k, c):
        arrived(k)
        return c

    lax.fori_loop(0, 16, arrive, 0)

    def exchange(stage, ref):
        @pl.when(y > 0)
        def _():
            border(stage, 0, ref.at[rows(3, 3)], ref.at[rows(19, 3)]).start()

        @pl.when(y < 3)
        def _():
            border(stage, 1, ref.at[rows(16, 3)], ref.at[rows(0, 3)]).start()

        wait_borders(stage, ref)

    exchange(1, x2)
    sweep(x2, ya, -2, 18)
    sweep(ya, yb, -1, 17)
    sweep(yb, x3, 0, 16)
    exchange(2, x3)
    sweep(x3, ya, -2, 18)
    sweep(ya, yb, -1, 17)

    def give(i):
        return remote(es.at[i], out.at[rows(i, 1), mine], g_send.at[i], g_recv.at[i], partner)

    def last_give(i, c):
        es[i] = one(yb, 8 * other + 2 + i)
        give(i).start()
        return c

    lax.fori_loop(0, 8, last_give, 0)

    def last_keep(i, c):
        out[rows(i, 1), mine] = one(yb, 8 * zh + 2 + i)
        return c

    lax.fori_loop(0, 8, last_keep, 0)

    def finish(i, c):
        remote(es.at[i], out.at[rows(i, 1), theirs], g_send.at[i], g_recv.at[i], partner).wait()
        return c

    lax.fori_loop(0, 8, finish, 0)
    swap_edge.wait_send()
    swap_rest.wait_send()

    @pl.when(edge_chip)
    def _():
        for far in range(2):
            remote(op.at[0], op.at[0], o_send.at[far], o_recv.at[0], partner).wait_send()

    def share_end(k, c):
        remote(op.at[0], op.at[0], o_send.at[1 + k], o_recv.at[0], partner).wait_send()
        return c

    lax.fori_loop(1, 8, share_end, 0)

    @pl.when(y > 0)
    def _():
        remote(op.at[pl.ds(2, 2)], op.at[pl.ds(18, 2)], o_send.at[9], o_recv.at[8], partner).wait_send()
        for stage in range(3):
            border(stage, 0, x1.at[rows(3, 3)], x1.at[rows(19, 3)]).wait_send()

    @pl.when(y < 3)
    def _():
        remote(op.at[pl.ds(16, 2)], op.at[pl.ds(0, 2)], o_send.at[10], o_recv.at[9], partner).wait_send()
        for stage in range(3):
            border(stage, 1, x1.at[rows(3, 3)], x1.at[rows(19, 3)]).wait_send()

    def sent(k, c):
        remote(ts.at[0], x2.at[rows(3, 1)], t_send.at[k], t_recv.at[0], partner).wait_send()
        return c

    lax.fori_loop(1, 16, sent, 0)

    @pl.when(jnp.logical_not(diagonal))
    def _():
        sent(0, 0)

    @pl.when(diagonal)
    def _():
        def passed(j, c):
            forward(j).wait_send()
            return c

        lax.fori_loop(0, 24, passed, 0)


def on_device(covariance, zonal, stencil):
    vmem, dma = pltpu.VMEM, pltpu.SemaphoreType.DMA
    return pl.pallas_call(
        kernel,
        out_shape=jax.ShapeDtypeStruct(covariance.shape, F32),
        in_specs=[pl.BlockSpec(memory_space=pltpu.VMEM)] * 3,
        out_specs=pl.BlockSpec(memory_space=pltpu.VMEM),
        scratch_shapes=[
            vmem((20, N + 8, N), F32),
            vmem((20, N, 3 * N), BF16),
            vmem((20, N, 3 * N), BF16),
            vmem((22 * N, N), F32),
            vmem((46 * N, N), F32),
            vmem((22 * N, N), F32),
            vmem((22 * N, N), F32),
            vmem((22 * N, N), F32),
            vmem((16, N, N), F32),
            vmem((8, N, N), F32),
            dma((2,)), dma((2,)), dma((11,)), dma((10,)), dma((6,)), dma((6,)),
            dma((16,)), dma((43,)), dma((24,)), dma((8,)), dma((8,)),
        ],
        compiler_params=pltpu.CompilerParams(
            collective_id=0, has_side_effects=True, vmem_limit_bytes=60 * 2**20),
        cost_estimate=pl.CostEstimate(flops=6_000_000_000, bytes_accessed=4 * 2**20, transcendentals=0),
        name="propagate",
    )(covariance, zonal, stencil)


def solution(mesh):
    placed = (P("rows", "cols"), P("rows", None, None), P("rows", None, None))
    return jax.shard_map(
        on_device, mesh=mesh, in_specs=placed, out_specs=P("rows", "cols"), check_vma=False
    )
```

time: 392 us -> 177 us (0.45)
  the two profiles are of different devices: /device:TPU:8 before, /device:TPU:41 now
where the time goes in v1:
time: 177 us
  Pallas kernels  173 us (98%)
  local copies, waits for them, and re-layouts  3.58 us (2%)
    pallas_call x1, Pallas kernels, on_device(): pl.pallas_call(kernel, out_shape=jax.ShapeDtypeStruct(covariance.shape, F...  173 us
    unnamed x2, local copies, waits for them, and re-layouts  3.58 us

profile of v1, /device:TPU:41, one launch (start us, length us, event | category | flops | bytes accessed | tf_op | source)
XLA Modules:
  0.0 177.1 jit_solution(1174984058718798787)
XLA Ops:
  0.0 1.3 copy.4.stencil
  1.3 173.5 %propagate.1 = f32[1024,256]{1,0:T(8,128)} custom-call(f32[1024,256]{1,0:T(8,128)} %cov.1, f32[8,128,128]{2,1,0:T(8,128)} %zonal.1, f32[8,3,128]{2,1,0:T(4,128)} %copy.4.stencil), custom_call_target="tpu_custom_call" | custom-call | flops 6000000000 | bytes 4194304 | tf_op jit(solution)/shard_map/propagate/pallas_call | solution.py:377
  174.8 2.3 %copy.6 = f32[1024,256]{1,0:T(8,128)} copy(f32[1024,256]{1,0:T(8,128)} %propagate.1) | data formatting | bytes 2097152

commit v2 on v1

--- a/solution.py
+++ b/solution.py
@@ -26,8 +26,8 @@
     return pl.ds(pl.multiple_of(first * N, N), count * N)
 
 
-def kernel(cov, zonal, stencil, out, op, b_hi, b_lo, x1, x2, x3, ya, yb, ts, es,
-           e_send, e_recv, o_send, o_recv, h_send, h_recv, t_send, t_recv, f_send, g_send, g_recv):
+def kernel(cov, zonal, stencil, out, op, z2, coef, x1, x2, x3, ya, yb, ts, es,
+           e_send, e_recv, o_send, o_recv, h_send, h_recv, z_send, z_recv, t_send, t_recv, f_send, g_send, g_recv):
     row, col = lax.axis_index("rows"), lax.axis_index("cols")
     y, zh = div(row, 2), rem(row, 2)
     x, zl, core = div(col, 8), div(rem(col, 8), 2), rem(col, 2)
@@ -38,7 +38,6 @@
     other = 1 - zh
     edge_chip = (zl == 0) | (zl == 3)
     diagonal = x == y
-    clat = zl * 4 + core * 2 + zh
 
     def remote(src, dst, send, recv, dev):
         return pltpu.make_async_remote_copy(
@@ -65,9 +64,12 @@
     def greet(dev):
         pl.semaphore_signal(barrier, inc=1, device_id=dev, device_id_type=MESH)
 
-    greet(partner)
-    near = jnp.where(zh == 0, jnp.where(zl < 2, 7, 4), jnp.where(zl < 2, 3, 0))
-    greet(device(x, y, near, core))
+    def greet_column(k, c):
+        d = rem(me16 + k, 16)
+        greet(device(x, y, div(d, 2), rem(d, 2)))
+        return c
+
+    lax.fori_loop(1, 16, greet_column, 0)
 
     def greet_group(k, c):
         q = rem(piece + k, 8)
@@ -86,30 +88,15 @@
 
     @pl.when(diagonal)
     def _():
-        def same(k, c):
-            d = rem(me16 + k, 16)
-            greet(device(x, y, div(d, 2), rem(d, 2)))
-            return c
-
-        lax.fori_loop(1, 16, same, 0)
-
-        def relayed(j, c):
-            greet(device(x, rem(x + 1 + div(j, 8), 4), rem(j, 8), 1 - core))
-            return c
-
-        lax.fori_loop(0, 24, relayed, 0)
+        for k in range(1, 4):
+            greet(device(x, rem(x + k, 4), z, core))
 
     @pl.when(jnp.logical_not(diagonal))
     def _():
-        def direct(k, c):
-            greet(device(y, x, k, core))
-            return c
-
-        lax.fori_loop(0, 8, direct, 0)
+        greet(device(y, x, z, core))
         greet(device(y, y, z, core))
 
-    writes = (1 + 7 + jnp.where(edge_chip, 2, 0) + jnp.where(y > 0, 1, 0) + jnp.where(y < 3, 1, 0)
-              + jnp.where(diagonal, 15 + 3, 16))
+    writes = 15 + 7 + jnp.where(y > 0, 1, 0) + jnp.where(y < 3, 1, 0) + jnp.where(diagonal, 3, 2)
     pl.semaphore_wait(barrier, writes)
 
     theirs = pl.ds(pl.multiple_of(other * N, N), N)
@@ -154,11 +141,11 @@
 
     def build(l, c):
         z_mat = op[l, 0:N, :]
-        for part, comp in enumerate((2, 0, 1)):
-            scaled = z_mat * op[l, N + comp:N + comp + 1, :]
-            hi = scaled.astype(BF16)
-            b_hi[l, :, part * N:(part + 1) * N] = hi
-            b_lo[l, :, part * N:(part + 1) * N] = (scaled - hi.astype(F32)).astype(BF16)
+        hi = z_mat.astype(BF16)
+        z2[l, :, 0:N] = hi
+        z2[l, :, N:2 * N] = (z_mat - hi.astype(F32)).astype(BF16)
+        for part in range(3):
+            coef[l, part] = jnp.broadcast_to(op[l, N + part:N + part + 1, :], (N, N)).T
         return c
 
     lax.fori_loop(2 + 8 * zh, 10 + 8 * zh, build, 0)
@@ -202,19 +189,20 @@
 
     def one(src, i):
         v = src[rows(i, 3), :]
+        v = coef[i, 0] * v[N:2 * N] + coef[i, 1] * v[2 * N:] + coef[i, 2] * v[0:N]
         hi = v.astype(BF16)
         lo = (v - hi.astype(F32)).astype(BF16)
-        bh = b_hi[i]
-        acc = jnp.dot(bh, lo, preferred_element_type=F32)
-        acc += jnp.dot(b_lo[i], hi, preferred_element_type=F32)
-        return acc + jnp.dot(bh, hi, preferred_element_type=F32)
-
-    def sweep(src, dst, first, last):
+        right = jnp.concatenate(
+            [jnp.concatenate([hi, hi], axis=0), jnp.concatenate([lo, jnp.zeros_like(lo)], axis=0)], axis=1)
+        both = jnp.dot(z2[i], right, preferred_element_type=F32)
+        return both[:, 0:N] + both[:, N:]
+
+    def sweep(src, dst, first, last, unroll):
         def body(i, c):
             dst[rows(i + 1, 1), :] = one(src, i)
             return c
 
-        lax.fori_loop(first + 2, last + 2, body, 0)
+        lax.fori_loop(first + 2, last + 2, body, 0, unroll=unroll)
 
     def wait_borders(stage, ref):
         @pl.when(y < 3)
@@ -227,65 +215,86 @@
 
     swap_rest.wait_recv()
     wait_borders(0, x1)
-    sweep(x1, ya, -2, 18)
-    sweep(ya, yb, -1, 17)
+    sweep(x1, ya, -2, 18, 5)
+    sweep(ya, yb, -1, 17, 6)
 
     def turn(lat, c):
         ts[lat] = one(yb, lat + 2).T
         return c
 
-    lax.fori_loop(0, 16, turn, 0)
-
-    def target(k):
-        d = rem(me16 + k, 16)
-        zt, ct = div(d, 2), rem(d, 2)
-        lat = 8 * div(rem(zt, 4), 2) + 4 * rem(zt, 2) + 2 * ct + div(zt, 4)
-        relay = jnp.logical_and(jnp.logical_not(diagonal), ct != core)
-        dev = device(jnp.where(relay, x, y), x, zt, ct)
-        slot = jnp.where(relay, 19 + rem(y + 3 - x, 4) * 8 + z, clat)
-        return lat, slot, dev
-
-    def send_block(k, c):
-        lat, slot, dev = target(k)
-        remote(ts.at[lat], x2.at[rows(slot + 3, 1)], t_send.at[k], t_recv.at[slot], dev).start()
-        return c
-
-    self_copy = pltpu.make_async_copy(
-        ts.at[8 * div(zl, 2) + 4 * rem(zl, 2) + 2 * core + zh], x2.at[rows(clat + 3, 1)], t_recv.at[clat])
+    lax.fori_loop(0, 16, turn, 0, unroll=8)
+
+    def order(i):
+        return jnp.where(rem(i, 2) == 1, div(i + 1, 2), jnp.where(i == 0, 0, 16 - div(i, 2)))
+
+    def block_of(d):
+        zt = div(d, 2)
+        return 8 * div(rem(zt, 4), 2) + 4 * rem(zt, 2) + 2 * rem(d, 2) + div(zt, 4)
+
+    def place(s):
+        return 3 + rem(div(s, 2), 4) * 4 + rem(s, 2) * 2 + div(s, 8)
+
+    def landing(s):
+        return rows(jnp.where(diagonal, place(s), 46 + s), 1)
+
+    self_copy = pltpu.make_async_copy(ts.at[block_of(me16)], x2.at[landing(me16)], z_recv.at[me16])
+    self_copy.start()
+
+    def column_send(i, c):
+        d = rem(me16 + order(i), 16)
+        remote(ts.at[block_of(d)], x2.at[landing(me16)], z_send.at[i], z_recv.at[me16],
+               device(x, y, div(d, 2), rem(d, 2))).start()
+        return c
+
+    lax.fori_loop(1, 16, column_send, 0)
+
+    def source(i):
+        return rem(me16 - order(i) + 16, 16)
+
+    def column_wait(i, c):
+        s = source(i)
+        remote(ts.at[0], x2.at[landing(s)], z_send.at[0], z_recv.at[s], partner).wait_recv()
+        return c
+
+    def onward(i):
+        s = source(i)
+        relay = rem(i, 2) == 1
+        slot = jnp.where(relay, 22 + rem(y + 3 - x, 4) * 8 + div(i, 2), place(s))
+        sem = jnp.where(relay, 16 + rem(y + 3 - x, 4) * 8 + div(i, 2), s)
+        return remote(x2.at[landing(s)], x2.at[rows(slot, 1)], t_send.at[i], t_recv.at[sem],
+                      device(jnp.where(relay, x, y), x, z, core))
+
+    def forward(j):
+        m, o = div(j, 3), rem(j, 3)
+        s = source(2 * m + 1)
+        return remote(x2.at[rows(22 + o * 8 + m, 1)], x2.at[rows(place(s), 1)], f_send.at[j], t_recv.at[s],
+                      device(rem(x + 1 + o, 4), x, z, core))
+
+    @pl.when(jnp.logical_not(diagonal))
+    def _():
+        def go(i, c):
+            column_wait(i, 0)
+            onward(i).start()
+            return c
+
+        lax.fori_loop(0, 16, go, 0)
+
+        def arrive(s, c):
+            remote(ts.at[0], x2.at[rows(place(s), 1)], z_send.at[0], t_recv.at[s], partner).wait_recv()
+            return c
+
+        lax.fori_loop(0, 16, arrive, 0)
 
     @pl.when(diagonal)
     def _():
-        self_copy.start()
-
-    @pl.when(jnp.logical_not(diagonal))
-    def _():
-        send_block(0, 0)
-
-    lax.fori_loop(1, 16, send_block, 0)
-
-    def forward(j):
-        zs = rem(j, 8)
-        lat_from = rem(zs, 4) * 4 + (1 - core) * 2 + div(zs, 4)
-        return remote(x2.at[rows(22 + j, 1)], x2.at[rows(lat_from + 3, 1)], f_send.at[j], t_recv.at[lat_from],
-                      device(rem(x + 1 + div(j, 8), 4), x, z, core))
-
-    def arrived(slot):
-        remote(ts.at[0], x2.at[rows(slot + 3, 1)], t_send.at[0], t_recv.at[slot], partner).wait_recv()
-
-    @pl.when(diagonal)
-    def _():
         def pass_on(j, c):
-            arrived(19 + j)
+            slot = rem(j, 3) * 8 + div(j, 3)
+            remote(ts.at[0], x2.at[rows(22 + slot, 1)], z_send.at[0], t_recv.at[16 + slot], partner).wait_recv()
             forward(j).start()
             return c
 
         lax.fori_loop(0, 24, pass_on, 0)
-
-    def arrive(k, c):
-        arrived(k)
-        return c
-
-    lax.fori_loop(0, 16, arrive, 0)
+        lax.fori_loop(0, 16, column_wait, 0)
 
     def exchange(stage, ref):
         @pl.when(y > 0)
@@ -299,12 +308,12 @@
         wait_borders(stage, ref)
 
     exchange(1, x2)
-    sweep(x2, ya, -2, 18)
-    sweep(ya, yb, -1, 17)
-    sweep(yb, x3, 0, 16)
+    sweep(x2, ya, -2, 18, 5)
+    sweep(ya, yb, -1, 17, 6)
+    sweep(yb, x3, 0, 16, 8)
     exchange(2, x3)
-    sweep(x3, ya, -2, 18)
-    sweep(ya, yb, -1, 17)
+    sweep(x3, ya, -2, 18, 5)
+    sweep(ya, yb, -1, 17, 6)
 
     def give(i):
         return remote(es.at[i], out.at[rows(i, 1), mine], g_send.at[i], g_recv.at[i], partner)
@@ -314,13 +323,13 @@
         give(i).start()
         return c
 
-    lax.fori_loop(0, 8, last_give, 0)
+    lax.fori_loop(0, 8, last_give, 0, unroll=4)
 
     def last_keep(i, c):
         out[rows(i, 1), mine] = one(yb, 8 * zh + 2 + i)
         return c
 
-    lax.fori_loop(0, 8, last_keep, 0)
+    lax.fori_loop(0, 8, last_keep, 0, unroll=4)
 
     def finish(i, c):
         remote(es.at[i], out.at[rows(i, 1), theirs], g_send.at[i], g_recv.at[i], partner).wait()
@@ -353,15 +362,19 @@
         for stage in range(3):
             border(stage, 1, x1.at[rows(3, 3)], x1.at[rows(19, 3)]).wait_send()
 
-    def sent(k, c):
-        remote(ts.at[0], x2.at[rows(3, 1)], t_send.at[k], t_recv.at[0], partner).wait_send()
+    def sent(i, c):
+        remote(ts.at[0], x2.at[rows(3, 1)], z_send.at[i], z_recv.at[0], partner).wait_send()
         return c
 
     lax.fori_loop(1, 16, sent, 0)
 
     @pl.when(jnp.logical_not(diagonal))
     def _():
-        sent(0, 0)
+        def gone(i, c):
+            onward(i).wait_send()
+            return c
+
+        lax.fori_loop(0, 16, gone, 0)
 
     @pl.when(diagonal)
     def _():
@@ -381,21 +394,21 @@
         out_specs=pl.BlockSpec(memory_space=pltpu.VMEM),
         scratch_shapes=[
             vmem((20, N + 8, N), F32),
-            vmem((20, N, 3 * N), BF16),
-            vmem((20, N, 3 * N), BF16),
+            vmem((20, N, 2 * N), BF16),
+            vmem((20, 3, N, N), F32),
             vmem((22 * N, N), F32),
-            vmem((46 * N, N), F32),
+            vmem((62 * N, N), F32),
             vmem((22 * N, N), F32),
             vmem((22 * N, N), F32),
             vmem((22 * N, N), F32),
             vmem((16, N, N), F32),
             vmem((8, N, N), F32),
             dma((2,)), dma((2,)), dma((11,)), dma((10,)), dma((6,)), dma((6,)),
-            dma((16,)), dma((43,)), dma((24,)), dma((8,)), dma((8,)),
+            dma((16,)), dma((16,)), dma((16,)), dma((40,)), dma((24,)), dma((8,)), dma((8,)),
         ],
         compiler_params=pltpu.CompilerParams(
             collective_id=0, has_side_effects=True, vmem_limit_bytes=60 * 2**20),
-        cost_estimate=pl.CostEstimate(flops=6_000_000_000, bytes_accessed=4 * 2**20, transcendentals=0),
+        cost_estimate=pl.CostEstimate(flops=2_000_000_000, bytes_accessed=4 * 2**20, transcendentals=0),
         name="propagate",
     )(covariance, zonal, stencil)
 

time: 177 us -> 136 us (0.77)
  the two profiles are of different devices: /device:TPU:41 before, /device:TPU:8 now
where the time goes in v2:
time: 136 us
  Pallas kernels  132 us (97%)
  local copies, waits for them, and re-layouts  3.58 us (3%)
    pallas_call x1, Pallas kernels, on_device(): pl.pallas_call(kernel, out_shape=jax.ShapeDtypeStruct(covariance.shape, F...  132 us
    unnamed x2, local copies, waits for them, and re-layouts  3.58 us

profile of v2, /device:TPU:8, one launch (start us, length us, event | category | flops | bytes accessed | tf_op | source)
XLA Modules:
  0.0 136.0 jit_solution(9542986557237267294)
XLA Ops:
  0.0 1.3 copy.4.stencil
  1.3 132.4 %propagate.1 = f32[1024,256]{1,0:T(8,128)} custom-call(f32[1024,256]{1,0:T(8,128)} %cov.1, f32[8,128,128]{2,1,0:T(8,128)} %zonal.1, f32[8,3,128]{2,1,0:T(4,128)} %copy.4.stencil), custom_call_target="tpu_custom_call" | custom-call | flops 2000000000 | bytes 4194304 | tf_op jit(solution)/shard_map/propagate/pallas_call | solution.py:390
  133.7 2.3 %copy.6 = f32[1024,256]{1,0:T(8,128)} copy(f32[1024,256]{1,0:T(8,128)} %propagate.1) | data formatting | bytes 2097152

commit v3 on v2

--- a/solution.py
+++ b/solution.py
@@ -36,7 +36,6 @@
     partner = (row + 1 - 2 * zh, col)
     piece = x * 2 + core
     other = 1 - zh
-    edge_chip = (zl == 0) | (zl == 3)
     diagonal = x == y
 
     def remote(src, dst, send, recv, dev):
@@ -106,13 +105,9 @@
     swap_rest = remote(cov.at[rows(other * 3, 5), theirs], x1.at[rows(6 + zh * 5, 5)],
                        e_send.at[1], e_recv.at[1], partner)
 
-    @pl.when(edge_chip)
-    def _():
-        for far in range(2):
-            to = jnp.where(zl == 3, rem(z + 1 + far, 8), rem(z + 7 - far, 8))
-            slot = 2 + 8 * zh + piece
-            remote(op.at[slot], op.at[slot], o_send.at[far], o_recv.at[piece], device(x, y, to, core)).start()
-
+    kept = 2 + 8 * zh + piece
+    gotten = 2 + 8 * other + piece
+    remote(op.at[kept], op.at[kept], o_send.at[0], o_recv.at[piece], partner).start()
     swap_edge.start()
     swap_rest.start()
 
@@ -128,16 +123,6 @@
         border(0, zh, cov.at[rows(zh * 5, 3), mine], x1.at[rows(19 - 19 * zh, 3)]).start()
 
     x1[rows(3 + 8 * zh, 8), :] = cov[:, mine]
-
-    slot = 2 + 8 * other + piece
-    remote(op.at[slot], op.at[slot], o_send.at[0], o_recv.at[piece], partner).wait_recv()
-
-    def share(k, c):
-        q = rem(piece + k, 8)
-        remote(op.at[slot], op.at[slot], o_send.at[1 + k], o_recv.at[piece], device(div(q, 2), y, z, rem(q, 2))).start()
-        return c
-
-    lax.fori_loop(1, 8, share, 0)
 
     def build(l, c):
         z_mat = op[l, 0:N, :]
@@ -150,11 +135,14 @@
 
     lax.fori_loop(2 + 8 * zh, 10 + 8 * zh, build, 0)
 
-    swap_edge.wait_recv()
-
-    @pl.when(has(other))
-    def _():
-        border(0, other, x1.at[rows(3 + 13 * other, 3)], x1.at[rows(19 - 19 * other, 3)]).start()
+    remote(op.at[gotten], op.at[gotten], o_send.at[0], o_recv.at[piece], partner).wait_recv()
+
+    def share(k, c):
+        q = rem(piece + k, 8)
+        remote(op.at[gotten], op.at[gotten], o_send.at[k], o_recv.at[piece], device(div(q, 2), y, z, rem(q, 2))).start()
+        return c
+
+    lax.fori_loop(1, 8, share, 0)
 
     def shared(k, c):
         q = rem(piece + k, 8)
@@ -173,6 +161,12 @@
     def _():
         remote(op.at[pl.ds(16, 2)], op.at[pl.ds(0, 2)], o_send.at[10], o_recv.at[9],
                device(x, y + 1, z, core)).start()
+
+    swap_edge.wait_recv()
+
+    @pl.when(has(other))
+    def _():
+        border(0, other, x1.at[rows(3 + 13 * other, 3)], x1.at[rows(19 - 19 * other, 3)]).start()
 
     lax.fori_loop(2 + 8 * other, 10 + 8 * other, build, 0)
 
@@ -305,15 +299,25 @@
         def _():
             border(stage, 1, ref.at[rows(16, 3)], ref.at[rows(0, 3)]).start()
 
-        wait_borders(stage, ref)
+    def edges(src, dst, first):
+        def body(k, c):
+            for i in (first + 2 + k, 15 - first + k):
+                dst[rows(i + 1, 1), :] = one(src, i)
+            return c
+
+        lax.fori_loop(0, 3, body, 0, unroll=3)
 
     exchange(1, x2)
-    sweep(x2, ya, -2, 18, 5)
-    sweep(ya, yb, -1, 17, 6)
-    sweep(yb, x3, 0, 16, 8)
+    sweep(x2, ya, 1, 15, 7)
+    sweep(ya, yb, 2, 14, 6)
+    sweep(yb, x3, 3, 13, 5)
+    wait_borders(1, x2)
+    edges(x2, ya, -2)
+    edges(ya, yb, -1)
+    edges(yb, x3, 0)
     exchange(2, x3)
-    sweep(x3, ya, -2, 18, 5)
-    sweep(ya, yb, -1, 17, 6)
+    sweep(x3, ya, 1, 15, 7)
+    sweep(ya, yb, 2, 14, 6)
 
     def give(i):
         return remote(es.at[i], out.at[rows(i, 1), mine], g_send.at[i], g_recv.at[i], partner)
@@ -323,7 +327,11 @@
         give(i).start()
         return c
 
-    lax.fori_loop(0, 8, last_give, 0, unroll=4)
+    lax.fori_loop(0, 5, lambda k, c: last_give(3 * zh + k, c), 0, unroll=5)
+    wait_borders(2, x3)
+    edges(x3, ya, -2)
+    edges(ya, yb, -1)
+    lax.fori_loop(0, 3, lambda k, c: last_give(5 * other + k, c), 0, unroll=3)
 
     def last_keep(i, c):
         out[rows(i, 1), mine] = one(yb, 8 * zh + 2 + i)
@@ -339,13 +347,10 @@
     swap_edge.wait_send()
     swap_rest.wait_send()
 
-    @pl.when(edge_chip)
-    def _():
-        for far in range(2):
-            remote(op.at[0], op.at[0], o_send.at[far], o_recv.at[0], partner).wait_send()
+    remote(op.at[0], op.at[0], o_send.at[0], o_recv.at[0], partner).wait_send()
 
     def share_end(k, c):
-        remote(op.at[0], op.at[0], o_send.at[1 + k], o_recv.at[0], partner).wait_send()
+        remote(op.at[0], op.at[0], o_send.at[k], o_recv.at[0], partner).wait_send()
         return c
 
     lax.fori_loop(1, 8, share_end, 0)

time: 136 us -> 120 us (0.88)
  the two profiles are of different devices: /device:TPU:8 before, /device:TPU:1 now
where the time goes in v3:
time: 120 us
  Pallas kernels  117 us (98%)
  local copies, waits for them, and re-layouts  3.58 us (3%)
    pallas_call x1, Pallas kernels, on_device(): pl.pallas_call(kernel, out_shape=jax.ShapeDtypeStruct(covariance.shape, F...  117 us
    unnamed x2, local copies, waits for them, and re-layouts  3.58 us

profile of v3, /device:TPU:1, one launch (start us, length us, event | category | flops | bytes accessed | tf_op | source)
XLA Modules:
  0.0 120.3 jit_solution(14284613070021414379)
XLA Ops:
  0.0 1.3 %copy.4.stencil = f32[8,3,128]{2,1,0:T(4,128)} copy(f32[8,3,128]{2,0,1:T(8,128)} %param.5) | data formatting | bytes 24576 | tf_op args[2]
  1.3 116.7 %propagate.1 = f32[1024,256]{1,0:T(8,128)} custom-call(f32[1024,256]{1,0:T(8,128)} %cov.1, f32[8,128,128]{2,1,0:T(8,128)} %zonal.1, f32[8,3,128]{2,1,0:T(4,128)} %copy.4.stencil), custom_call_target="tpu_custom_call" | custom-call | flops 2000000000 | bytes 4194304 | tf_op jit(solution)/shard_map/propagate/pallas_call | solution.py:395
  118.0 2.3 %copy.6 = f32[1024,256]{1,0:T(8,128)} copy(f32[1024,256]{1,0:T(8,128)} %propagate.1) | data formatting | bytes 2097152

commit v4 on v3

--- a/solution.py
+++ b/solution.py
@@ -26,7 +26,7 @@
     return pl.ds(pl.multiple_of(first * N, N), count * N)
 
 
-def kernel(cov, zonal, stencil, out, op, z2, coef, x1, x2, x3, ya, yb, ts, es,
+def kernel(cov, zonal, stencil, out, op, z2, coef, x1, x2, x3, ya, yb, s4, s5, ts, es,
            e_send, e_recv, o_send, o_recv, h_send, h_recv, z_send, z_recv, t_send, t_recv, f_send, g_send, g_recv):
     row, col = lax.axis_index("rows"), lax.axis_index("cols")
     y, zh = div(row, 2), rem(row, 2)
@@ -42,9 +42,10 @@
         return pltpu.make_async_remote_copy(
             src_ref=src, dst_ref=dst, send_sem=send, recv_sem=recv, device_id=dev, device_id_type=MESH)
 
+    op[pl.ds(2 + 8 * zh, 8), 0:N, :] = zonal[...]
     for i in range(8):
-        op[2 + 8 * zh + i, 0:N, :] = zonal[i]
-        op[2 + 8 * zh + i, N:N + 3, :] = stencil[i]
+        for part in range(3):
+            op[2 + 8 * zh + i, N + part:N + part + 1, :] = stencil[part, i:i + 1, :]
 
     @pl.when(y == 0)
     def _():
@@ -252,7 +253,7 @@
 
     def onward(i):
         s = source(i)
-        relay = rem(i, 2) == 1
+        relay = rem(i, 2) == 0
         slot = jnp.where(relay, 22 + rem(y + 3 - x, 4) * 8 + div(i, 2), place(s))
         sem = jnp.where(relay, 16 + rem(y + 3 - x, 4) * 8 + div(i, 2), s)
         return remote(x2.at[landing(s)], x2.at[rows(slot, 1)], t_send.at[i], t_recv.at[sem],
@@ -260,7 +261,7 @@
 
     def forward(j):
         m, o = div(j, 3), rem(j, 3)
-        s = source(2 * m + 1)
+        s = source(2 * m)
         return remote(x2.at[rows(22 + o * 8 + m, 1)], x2.at[rows(place(s), 1)], f_send.at[j], t_recv.at[s],
                       device(rem(x + 1 + o, 4), x, z, core))
 
@@ -307,36 +308,37 @@
 
         lax.fori_loop(0, 3, body, 0, unroll=3)
 
+    def give(i):
+        return remote(es.at[i], out.at[rows(i, 1), mine], g_send.at[i], g_recv.at[i], partner)
+
+    def last_give(i, c):
+        es[i] = one(s5, 8 * other + 2 + i)
+        give(i).start()
+        return c
+
+    def last_keep(i, c):
+        out[rows(i, 1), mine] = one(s5, 8 * zh + 2 + i)
+        return c
+
     exchange(1, x2)
     sweep(x2, ya, 1, 15, 7)
     sweep(ya, yb, 2, 14, 6)
     sweep(yb, x3, 3, 13, 5)
+    sweep(x3, s4, 4, 12, 8)
+    sweep(s4, s5, 5, 11, 6)
+    lax.fori_loop(0, 2, lambda k, c: last_give(6 * zh + k, c), 0, unroll=2)
     wait_borders(1, x2)
     edges(x2, ya, -2)
     edges(ya, yb, -1)
     edges(yb, x3, 0)
     exchange(2, x3)
-    sweep(x3, ya, 1, 15, 7)
-    sweep(ya, yb, 2, 14, 6)
-
-    def give(i):
-        return remote(es.at[i], out.at[rows(i, 1), mine], g_send.at[i], g_recv.at[i], partner)
-
-    def last_give(i, c):
-        es[i] = one(yb, 8 * other + 2 + i)
-        give(i).start()
-        return c
-
-    lax.fori_loop(0, 5, lambda k, c: last_give(3 * zh + k, c), 0, unroll=5)
+    edges(x3, s4, 1)
+    edges(s4, s5, 2)
+    lax.fori_loop(0, 3, lambda k, c: last_give(2 + zh + k, c), 0, unroll=3)
     wait_borders(2, x3)
-    edges(x3, ya, -2)
-    edges(ya, yb, -1)
+    edges(x3, s4, -2)
+    edges(s4, s5, -1)
     lax.fori_loop(0, 3, lambda k, c: last_give(5 * other + k, c), 0, unroll=3)
-
-    def last_keep(i, c):
-        out[rows(i, 1), mine] = one(yb, 8 * zh + 2 + i)
-        return c
-
     lax.fori_loop(0, 8, last_keep, 0, unroll=4)
 
     def finish(i, c):
@@ -406,16 +408,18 @@
             vmem((22 * N, N), F32),
             vmem((22 * N, N), F32),
             vmem((22 * N, N), F32),
+            vmem((22 * N, N), F32),
+            vmem((22 * N, N), F32),
             vmem((16, N, N), F32),
             vmem((8, N, N), F32),
             dma((2,)), dma((2,)), dma((11,)), dma((10,)), dma((6,)), dma((6,)),
             dma((16,)), dma((16,)), dma((16,)), dma((40,)), dma((24,)), dma((8,)), dma((8,)),
         ],
         compiler_params=pltpu.CompilerParams(
-            collective_id=0, has_side_effects=True, vmem_limit_bytes=60 * 2**20),
+            collective_id=0, has_side_effects=True, vmem_limit_bytes=36 * 2**20),
         cost_estimate=pl.CostEstimate(flops=2_000_000_000, bytes_accessed=4 * 2**20, transcendentals=0),
         name="propagate",
-    )(covariance, zonal, stencil)
+    )(covariance, zonal, jnp.transpose(stencil, (1, 0, 2)))
 
 
 def solution(mesh):

time: 120 us -> 113 us (0.942)
  the two profiles are of different devices: /device:TPU:1 before, /device:TPU:8 now
where the time goes in v4:
time: 113 us; the launch traced here: 112 us
  Pallas kernels  108 us (96%)
  local copies, waits for them, and re-layouts  3.94 us (3%)
    pallas_call x1, Pallas kernels, on_device(): pl.pallas_call(kernel, out_shape=jax.ShapeDtypeStruct(covariance.shape, F...  108 us
    unnamed x7, local copies, waits for them, and re-layouts  3.94 us

profile of v4, /device:TPU:8, one launch (start us, length us, event | category | flops | bytes accessed | tf_op | source)
XLA Modules:
  0.0 112.3 jit_solution(16513001956203366472)
XLA Ops:
  0.0 0.0 copy-start
  0.0 1.2 %copy-done = f32[1024,256]{1,0:T(8,128)S(1)} copy-done((f32[1024,256]{1,0:T(8,128)S(1)}, f32[1024,256]{1,0:T(8,128)}, u32[]{:S(2)}) %copy-start) | copy-done | bytes 1048600
  1.2 0.0 copy-start.1
  1.2 1.0 copy-done.1
  2.3 0.0 copy-start.2
  2.3 0.7 copy-done.2
  3.0 108.3 %propagate.1 = f32[1024,256]{1,0:T(8,128)S(1)} custom-call(f32[1024,256]{1,0:T(8,128)S(1)} %copy-done, f32[8,128,128]{2,1,0:T(8,128)S(1)} %copy-done.1, f32[3,8,128]{2,1,0:T(8,128)S(1)} %bitcast.1), custom_call_target="tpu_custom_call" | custom-call | flops 2000000000 | bytes 4194304 | tf_op jit(solution)/shard_map/propagate/pallas_call | solution.py:397
  111.3 1.0 copy.5
Async XLA Ops:
  0.0 1.2 %copy-start = (f32[1024,256]{1,0:T(8,128)S(1)}, f32[1024,256]{1,0:T(8,128)}, u32[]{:S(2)}) copy-start(f32[1024,256]{1,0:T(8,128)} %cov.1) | copy-start | bytes 3145732
  1.2 1.0 copy-start.1
  2.3 0.7 copy-start.2

commit v5 on v4

--- a/solution.py
+++ b/solution.py
@@ -26,8 +26,8 @@
     return pl.ds(pl.multiple_of(first * N, N), count * N)
 
 
-def kernel(cov, zonal, stencil, out, op, z2, coef, x1, x2, x3, ya, yb, s4, s5, ts, es,
-           e_send, e_recv, o_send, o_recv, h_send, h_recv, z_send, z_recv, t_send, t_recv, f_send, g_send, g_recv):
+def kernel(cov, zonal, stencil, out, st, op, z2, coef, x1, x2, x3, ya, yb, s4, s5, ts, es,
+           l_sem, e_send, e_recv, o_send, o_recv, h_send, h_recv, z_send, z_recv, t_send, t_recv, f_send, g_send, g_recv):
     row, col = lax.axis_index("rows"), lax.axis_index("cols")
     y, zh = div(row, 2), rem(row, 2)
     x, zl, core = div(col, 8), div(rem(col, 8), 2), rem(col, 2)
@@ -42,10 +42,57 @@
         return pltpu.make_async_remote_copy(
             src_ref=src, dst_ref=dst, send_sem=send, recv_sem=recv, device_id=dev, device_id_type=MESH)
 
-    op[pl.ds(2 + 8 * zh, 8), 0:N, :] = zonal[...]
+    theirs = pl.ds(pl.multiple_of(other * N, N), N)
+    mine = pl.ds(pl.multiple_of(zh * N, N), N)
+    load_stencil = pltpu.make_async_copy(stencil, st, l_sem.at[0])
+    load_zonal = pltpu.make_async_copy(zonal, op.at[pl.ds(2 + 8 * zh, 8), 0:N, :], l_sem.at[1])
+    load_own = pltpu.make_async_copy(cov.at[:, mine], x1.at[rows(3 + 8 * zh, 8)], l_sem.at[2])
+    load_stencil.start()
+    load_zonal.start()
+    load_own.start()
+
+    barrier = pltpu.get_barrier_semaphore()
+
+    def greet(dev):
+        pl.semaphore_signal(barrier, inc=1, device_id=dev, device_id_type=MESH)
+
+    def greet_column(k, c):
+        d = rem(me16 + k, 16)
+        greet(device(x, y, div(d, 2), rem(d, 2)))
+        return c
+
+    lax.fori_loop(1, 16, greet_column, 0)
+
+    def greet_group(k, c):
+        q = rem(piece + k, 8)
+        greet(device(div(q, 2), y, z, rem(q, 2)))
+        return c
+
+    lax.fori_loop(1, 8, greet_group, 0)
+
+    @pl.when(y > 0)
+    def _():
+        greet(device(x, y - 1, z, core))
+
+    @pl.when(y < 3)
+    def _():
+        greet(device(x, y + 1, z, core))
+
+    @pl.when(diagonal)
+    def _():
+        for k in range(1, 4):
+            greet(device(x, rem(x + k, 4), z, core))
+
+    @pl.when(jnp.logical_not(diagonal))
+    def _():
+        greet(device(y, x, z, core))
+        greet(device(y, y, z, core))
+
+    load_stencil.wait()
+    load_zonal.wait()
     for i in range(8):
         for part in range(3):
-            op[2 + 8 * zh + i, N + part:N + part + 1, :] = stencil[part, i:i + 1, :]
+            op[2 + 8 * zh + i, N + part:N + part + 1, :] = st[part, i:i + 1, :]
 
     @pl.when(y == 0)
     def _():
@@ -59,48 +106,9 @@
         for ref in (x1, x2, x3):
             ref[19 * N:22 * N, :] = jnp.zeros((3 * N, N), F32)
 
-    barrier = pltpu.get_barrier_semaphore()
-
-    def greet(dev):
-        pl.semaphore_signal(barrier, inc=1, device_id=dev, device_id_type=MESH)
-
-    def greet_column(k, c):
-        d = rem(me16 + k, 16)
-        greet(device(x, y, div(d, 2), rem(d, 2)))
-        return c
-
-    lax.fori_loop(1, 16, greet_column, 0)
-
-    def greet_group(k, c):
-        q = rem(piece + k, 8)
-        greet(device(div(q, 2), y, z, rem(q, 2)))
-        return c
-
-    lax.fori_loop(1, 8, greet_group, 0)
-
-    @pl.when(y > 0)
-    def _():
-        greet(device(x, y - 1, z, core))
-
-    @pl.when(y < 3)
-    def _():
-        greet(device(x, y + 1, z, core))
-
-    @pl.when(diagonal)
-    def _():
-        for k in range(1, 4):
-            greet(device(x, rem(x + k, 4), z, core))
-
-    @pl.when(jnp.logical_not(diagonal))
-    def _():
-        greet(device(y, x, z, core))
-        greet(device(y, y, z, core))
-
     writes = 15 + 7 + jnp.where(y > 0, 1, 0) + jnp.where(y < 3, 1, 0) + jnp.where(diagonal, 3, 2)
     pl.semaphore_wait(barrier, writes)
 
-    theirs = pl.ds(pl.multiple_of(other * N, N), N)
-    mine = pl.ds(pl.multiple_of(zh * N, N), N)
     swap_edge = remote(cov.at[rows(zh * 5, 3), theirs], x1.at[rows(3 + zh * 13, 3)],
                        e_send.at[0], e_recv.at[0], partner)
     swap_rest = remote(cov.at[rows(other * 3, 5), theirs], x1.at[rows(6 + zh * 5, 5)],
@@ -122,8 +130,6 @@
     @pl.when(has(zh))
     def _():
         border(0, zh, cov.at[rows(zh * 5, 3), mine], x1.at[rows(19 - 19 * zh, 3)]).start()
-
-    x1[rows(3 + 8 * zh, 8), :] = cov[:, mine]
 
     def build(l, c):
         z_mat = op[l, 0:N, :]
@@ -208,6 +214,7 @@
         def _():
             border(stage, 1, ref.at[rows(0, 3)], ref.at[rows(0, 3)]).wait_recv()
 
+    load_own.wait()
     swap_rest.wait_recv()
     wait_borders(0, x1)
     sweep(x1, ya, -2, 18, 5)
@@ -397,9 +404,10 @@
     return pl.pallas_call(
         kernel,
         out_shape=jax.ShapeDtypeStruct(covariance.shape, F32),
-        in_specs=[pl.BlockSpec(memory_space=pltpu.VMEM)] * 3,
+        in_specs=[pl.BlockSpec(memory_space=pltpu.HBM)] * 3,
         out_specs=pl.BlockSpec(memory_space=pltpu.VMEM),
         scratch_shapes=[
+            vmem((3, 8, N), F32),
             vmem((20, N + 8, N), F32),
             vmem((20, N, 2 * N), BF16),
             vmem((20, 3, N, N), F32),
@@ -412,14 +420,14 @@
             vmem((22 * N, N), F32),
             vmem((16, N, N), F32),
             vmem((8, N, N), F32),
-            dma((2,)), dma((2,)), dma((11,)), dma((10,)), dma((6,)), dma((6,)),
+            dma((3,)), dma((2,)), dma((2,)), dma((11,)), dma((10,)), dma((6,)), dma((6,)),
             dma((16,)), dma((16,)), dma((16,)), dma((40,)), dma((24,)), dma((8,)), dma((8,)),
         ],
         compiler_params=pltpu.CompilerParams(
             collective_id=0, has_side_effects=True, vmem_limit_bytes=36 * 2**20),
         cost_estimate=pl.CostEstimate(flops=2_000_000_000, bytes_accessed=4 * 2**20, transcendentals=0),
         name="propagate",
-    )(covariance, zonal, jnp.transpose(stencil, (1, 0, 2)))
+    )(*(pltpu.with_memory_space_constraint(a, pltpu.HBM) for a in (covariance, zonal, jnp.transpose(stencil, (1, 0, 2)))))
 
 
 def solution(mesh):

time: 113 us -> 109 us (0.965)
  local copies, waits for them, and re-layouts: 3.94 us -> 0.97 us
    unnamed x7 -> x1, local copies, waits for them, and re-layouts: 3.94 us -> 0.97 us
where the time goes in v5:
time: 109 us
  Pallas kernels  108 us (99%)
    pallas_call x1, Pallas kernels, on_device(): pl.pallas_call(kernel, out_shape=jax.ShapeDtypeStruct(covariance.shape, F...  108 us

profile of v5, /device:TPU:8, one launch (start us, length us, event | category | flops | bytes accessed | tf_op | source)
XLA Modules:
  0.0 109.1 jit_solution(14558228814150800845)
XLA Ops:
  0.0 108.1 %propagate.1 = f32[1024,256]{1,0:T(8,128)S(1)} custom-call(f32[1024,256]{1,0:T(8,128)} %cov.1, f32[8,128,128]{2,1,0:T(8,128)} %zonal.1, f32[3,8,128]{2,1,0:T(8,128)} %bitcast.1), custom_call_target="tpu_custom_call" | custom-call | flops 2000000000 | bytes 4194304 | tf_op jit(solution)/shard_map/propagate/pallas_call | solution.py:404
  108.1 1.0 copy.5

commit v6 on v5

--- a/solution.py
+++ b/solution.py
@@ -214,18 +214,6 @@
         def _():
             border(stage, 1, ref.at[rows(0, 3)], ref.at[rows(0, 3)]).wait_recv()
 
-    load_own.wait()
-    swap_rest.wait_recv()
-    wait_borders(0, x1)
-    sweep(x1, ya, -2, 18, 5)
-    sweep(ya, yb, -1, 17, 6)
-
-    def turn(lat, c):
-        ts[lat] = one(yb, lat + 2).T
-        return c
-
-    lax.fori_loop(0, 16, turn, 0, unroll=8)
-
     def order(i):
         return jnp.where(rem(i, 2) == 1, div(i + 1, 2), jnp.where(i == 0, 0, 16 - div(i, 2)))
 
@@ -239,16 +227,64 @@
     def landing(s):
         return rows(jnp.where(diagonal, place(s), 46 + s), 1)
 
-    self_copy = pltpu.make_async_copy(ts.at[block_of(me16)], x2.at[landing(me16)], z_recv.at[me16])
-    self_copy.start()
-
-    def column_send(i, c):
-        d = rem(me16 + order(i), 16)
-        remote(ts.at[block_of(d)], x2.at[landing(me16)], z_send.at[i], z_recv.at[me16],
-               device(x, y, div(d, 2), rem(d, 2))).start()
-        return c
-
-    lax.fori_loop(1, 16, column_send, 0)
+    def place_of(lat):
+        return (4 * rem(lat, 2) + 2 * div(lat, 8) + rem(div(lat, 4), 2)) * 2 + rem(div(lat, 2), 2)
+
+    def column_send(lat, c):
+        d = place_of(lat)
+
+        @pl.when(d == me16)
+        def _():
+            pltpu.make_async_copy(ts.at[lat], x2.at[landing(me16)], z_recv.at[me16]).start()
+
+        @pl.when(d != me16)
+        def _():
+            remote(ts.at[lat], x2.at[landing(me16)], z_send.at[lat], z_recv.at[me16],
+                   device(x, y, div(d, 2), rem(d, 2))).start()
+
+        return c
+
+    def span(src, dst, first, count):
+        def body(k, c):
+            dst[rows(first + k + 1, 1), :] = one(src, first + k)
+            return c
+
+        lax.fori_loop(0, count, body, 0, unroll=count)
+
+    def turn(first, count):
+        def body(k, c):
+            ts[first - 2 + k] = one(yb, first + k).T
+            return c
+
+        lax.fori_loop(0, count, body, 0, unroll=count)
+
+    def wait_border(side):
+        border(0, side, x1.at[rows(19 - 19 * side, 3)], x1.at[rows(19 - 19 * side, 3)]).wait_recv()
+
+    load_own.wait()
+
+    @pl.when(has(zh))
+    def _():
+        wait_border(other)
+
+    span(x1, ya, 11 * zh, 9)
+    span(ya, yb, 1 + 11 * zh, 7)
+    turn(2 + 11 * zh, 5)
+
+    swap_rest.wait_recv()
+
+    @pl.when(has(other))
+    def _():
+        wait_border(zh)
+
+    span(x1, ya, 9 * other, 11)
+    span(ya, yb, 1 + 7 * other, 11)
+    turn(2 + 5 * other, 11)
+
+    def remaining(i, c):
+        return column_send(block_of(rem(me16 + order(i), 16)), c)
+
+    lax.fori_loop(0, 16, remaining, 0)
 
     def source(i):
         return rem(me16 - order(i) + 16, 16)
@@ -376,11 +412,14 @@
         for stage in range(3):
             border(stage, 1, x1.at[rows(3, 3)], x1.at[rows(19, 3)]).wait_send()
 
-    def sent(i, c):
-        remote(ts.at[0], x2.at[rows(3, 1)], z_send.at[i], z_recv.at[0], partner).wait_send()
-        return c
-
-    lax.fori_loop(1, 16, sent, 0)
+    def sent(lat, c):
+        @pl.when(place_of(lat) != me16)
+        def _():
+            remote(ts.at[0], x2.at[rows(3, 1)], z_send.at[lat], z_recv.at[0], partner).wait_send()
+
+        return c
+
+    lax.fori_loop(0, 16, sent, 0)
 
     @pl.when(jnp.logical_not(diagonal))
     def _():

time: 109 us -> 107 us (0.982)
  Pallas kernels: 108 us -> 105 us
    pallas_call x1, Pallas kernels: 108 us -> 105 us  [on_device(): pl.pallas_call(kernel, out_shape=jax.ShapeDtypeStruct(covariance.shape, F...]
where the time goes in v6:
time: 107 us; the launch traced here: 106 us
  Pallas kernels  105 us (98%)
    pallas_call x1, Pallas kernels, on_device(): pl.pallas_call(kernel, out_shape=jax.ShapeDtypeStruct(covariance.shape, F...  105 us

profile of v6, /device:TPU:8, one launch (start us, length us, event | category | flops | bytes accessed | tf_op | source)
XLA Modules:
  0.0 106.4 jit_solution(10247643767006470444)
XLA Ops:
  0.0 105.4 %propagate.1 = f32[1024,256]{1,0:T(8,128)S(1)} custom-call(f32[1024,256]{1,0:T(8,128)} %cov.1, f32[8,128,128]{2,1,0:T(8,128)} %zonal.1, f32[3,8,128]{2,1,0:T(8,128)} %bitcast.1), custom_call_target="tpu_custom_call" | custom-call | flops 2000000000 | bytes 4194304 | tf_op jit(solution)/shard_map/propagate/pallas_call | solution.py:443
  105.4 1.0 copy.5

commit v7 on v6

--- a/solution.py
+++ b/solution.py
@@ -37,6 +37,7 @@
     piece = x * 2 + core
     other = 1 - zh
     diagonal = x == y
+    near = rem(x + y, 2) == 1
 
     def remote(src, dst, send, recv, dev):
         return pltpu.make_async_remote_copy(
@@ -80,13 +81,12 @@
 
     @pl.when(diagonal)
     def _():
-        for k in range(1, 4):
+        for k in (1, 3):
             greet(device(x, rem(x + k, 4), z, core))
 
     @pl.when(jnp.logical_not(diagonal))
     def _():
-        greet(device(y, x, z, core))
-        greet(device(y, y, z, core))
+        greet(device(y, jnp.where(near, y, x), z, core))
 
     load_stencil.wait()
     load_zonal.wait()
@@ -106,7 +106,7 @@
         for ref in (x1, x2, x3):
             ref[19 * N:22 * N, :] = jnp.zeros((3 * N, N), F32)
 
-    writes = 15 + 7 + jnp.where(y > 0, 1, 0) + jnp.where(y < 3, 1, 0) + jnp.where(diagonal, 3, 2)
+    writes = 15 + 7 + jnp.where(y > 0, 1, 0) + jnp.where(y < 3, 1, 0) + jnp.where(diagonal, 2, 1)
     pl.semaphore_wait(barrier, writes)
 
     swap_edge = remote(cov.at[rows(zh * 5, 3), theirs], x1.at[rows(3 + zh * 13, 3)],
@@ -225,7 +225,7 @@
         return 3 + rem(div(s, 2), 4) * 4 + rem(s, 2) * 2 + div(s, 8)
 
     def landing(s):
-        return rows(jnp.where(diagonal, place(s), 46 + s), 1)
+        return rows(jnp.where(diagonal, place(s), 54 + s), 1)
 
     def place_of(lat):
         return (4 * rem(lat, 2) + 2 * div(lat, 8) + rem(div(lat, 4), 2)) * 2 + rem(div(lat, 2), 2)
@@ -296,17 +296,17 @@
 
     def onward(i):
         s = source(i)
-        relay = rem(i, 2) == 0
-        slot = jnp.where(relay, 22 + rem(y + 3 - x, 4) * 8 + div(i, 2), place(s))
-        sem = jnp.where(relay, 16 + rem(y + 3 - x, 4) * 8 + div(i, 2), s)
+        way = div(rem(y + 3 - x, 4), 2) * 16 + i
+        slot = jnp.where(near, 22 + way, place(s))
+        sem = jnp.where(near, 16 + way, s)
         return remote(x2.at[landing(s)], x2.at[rows(slot, 1)], t_send.at[i], t_recv.at[sem],
-                      device(jnp.where(relay, x, y), x, z, core))
+                      device(jnp.where(near, x, y), x, z, core))
 
     def forward(j):
-        m, o = div(j, 3), rem(j, 3)
-        s = source(2 * m)
-        return remote(x2.at[rows(22 + o * 8 + m, 1)], x2.at[rows(place(s), 1)], f_send.at[j], t_recv.at[s],
-                      device(rem(x + 1 + o, 4), x, z, core))
+        i, o = div(j, 2), rem(j, 2)
+        s = source(i)
+        return remote(x2.at[rows(22 + o * 16 + i, 1)], x2.at[rows(place(s), 1)], f_send.at[j], t_recv.at[s],
+                      device(rem(x + 1 + 2 * o, 4), x, z, core))
 
     @pl.when(jnp.logical_not(diagonal))
     def _():
@@ -326,12 +326,12 @@
     @pl.when(diagonal)
     def _():
         def pass_on(j, c):
-            slot = rem(j, 3) * 8 + div(j, 3)
+            slot = rem(j, 2) * 16 + div(j, 2)
             remote(ts.at[0], x2.at[rows(22 + slot, 1)], z_send.at[0], t_recv.at[16 + slot], partner).wait_recv()
             forward(j).start()
             return c
 
-        lax.fori_loop(0, 24, pass_on, 0)
+        lax.fori_loop(0, 32, pass_on, 0)
         lax.fori_loop(0, 16, column_wait, 0)
 
     def exchange(stage, ref):
@@ -435,7 +435,7 @@
             forward(j).wait_send()
             return c
 
-        lax.fori_loop(0, 24, passed, 0)
+        lax.fori_loop(0, 32, passed, 0)
 
 
 def on_device(covariance, zonal, stencil):
@@ -451,7 +451,7 @@
             vmem((20, N, 2 * N), BF16),
             vmem((20, 3, N, N), F32),
             vmem((22 * N, N), F32),
-            vmem((62 * N, N), F32),
+            vmem((70 * N, N), F32),
             vmem((22 * N, N), F32),
             vmem((22 * N, N), F32),
             vmem((22 * N, N), F32),
@@ -460,7 +460,7 @@
             vmem((16, N, N), F32),
             vmem((8, N, N), F32),
             dma((3,)), dma((2,)), dma((2,)), dma((11,)), dma((10,)), dma((6,)), dma((6,)),
-            dma((16,)), dma((16,)), dma((16,)), dma((40,)), dma((24,)), dma((8,)), dma((8,)),
+            dma((16,)), dma((16,)), dma((16,)), dma((48,)), dma((32,)), dma((8,)), dma((8,)),
         ],
         compiler_params=pltpu.CompilerParams(
             collective_id=0, has_side_effects=True, vmem_limit_bytes=36 * 2**20),

time: 107 us -> 106 us (level)
  no operation moved by 1% of the time
where the time goes in v7:
time: 106 us
  Pallas kernels  105 us (99%)
    pallas_call x1, Pallas kernels, on_device(): pl.pallas_call(kernel, out_shape=jax.ShapeDtypeStruct(covariance.shape, F...  105 us

profile of v7, /device:TPU:8, one launch (start us, length us, event | category | flops | bytes accessed | tf_op | source)
XLA Modules:
  0.0 105.6 jit_solution(16934914116520082165)
XLA Ops:
  0.0 104.6 %propagate.1 = f32[1024,256]{1,0:T(8,128)S(1)} custom-call(f32[1024,256]{1,0:T(8,128)} %cov.1, f32[8,128,128]{2,1,0:T(8,128)} %zonal.1, f32[3,8,128]{2,1,0:T(8,128)} %bitcast.1), custom_call_target="tpu_custom_call" | custom-call | flops 2000000000 | bytes 4194304 | tf_op jit(solution)/shard_map/propagate/pallas_call | solution.py:443
  104.6 1.0 copy.5
